TPU v7x, 32 devices: a whole 2x2x4 slice. The times are simulated.
32 devices in a mesh: rep: 2 (over y), sample: 4 (over z), head: 4 (over x, core).
Axes of the slice: x: 2, y: 2, z: 4, core: 2. Of those that a mesh axis runs over, the one named last changes fastest.
Arguments:
- x_pre: bfloat16 [8, 128, 8192], P(('rep', 'sample'), None, 'head'), parts along dimension 0, may hold values from -120 to 120
- z_pre: bfloat16 [8, 128, 8192], P(('rep', 'sample'), None, 'head'), parts along dimension 0, may hold values from -6 to 6
- b_pre: bfloat16 [8, 128, 512], P(('rep', 'sample')), parts along dimension 0, may hold values from -1.796875 to 1.796875
- c_pre: bfloat16 [8, 128, 512], P(('rep', 'sample')), parts along dimension 0, may hold values from -0.5390625 to 0.5390625
- dt_pre: float32 [8, 128, 128], P(('rep', 'sample'), None, 'head'), parts along dimension 0, may hold values from -1.5 to 7.5
- lengths: int32 [8], P(('rep', 'sample')), parts along dimension 0, may hold values from 64 to 128, as said below
- init_state: float32 [8, 128, 8192], P(('rep', 'sample'), None, 'head'), parts along dimension 0, may hold values from -6 to 6
- a_rates: float32 [128], P('head'), may hold values from 0.005 to 0.3
- dt_bias: float32 [128], P('head'), may hold values from -2 to -1
- skip_scale: float32 [128], P('head'), may hold values from 0.5 to 2
- norm_gain: float32 [8192], P('head'), may hold values from 0.5 to 1.5
- x_dec: bfloat16 [8, 4, 8192], P(('rep', 'sample'), None, 'head'), parts along dimension 0, may hold values from -120 to 120
- z_dec: bfloat16 [8, 4, 8192], P(('rep', 'sample'), None, 'head'), parts along dimension 0, may hold values from -6 to 6
- b_dec: bfloat16 [8, 4, 512], P(('rep', 'sample')), parts along dimension 0, may hold values from -6 to 6
- c_dec: bfloat16 [8, 4, 512], P(('rep', 'sample')), parts along dimension 0, may hold values from -0.5390625 to 0.5390625
- dt_dec: float32 [8, 4, 128], P(('rep', 'sample'), None, 'head'), parts along dimension 0, may hold values from -3 to 3
Outputs:
- out_pre: bfloat16 [8, 128, 8192], P(('rep', 'sample'), None, 'head'), parts along dimension 0
- final_state: bfloat16 [8, 128, 8192], P(('rep', 'sample'), None, 'head'), parts along dimension 0
- out_dec: bfloat16 [8, 4, 8192], P(('rep', 'sample'), None, 'head'), parts along dimension 0
There are 2 independent parts, one for each index of `rep`. A program takes and returns all parts, laid end to end along the dimension named above; an argument that names none is the same for every part. Nothing has to cross between parts.
Inputs may be any that keep to these rules, and one draw needn't show every extreme that they name: Each prompt's valid tokens are the first lengths[p] of its 128 positions; some prompt uses all 128.
All inputs are finite; a program needn't handle non-finite values.
Results may differ from a plain program's by a relative error of at most 0.006.
Values may be sent and summed in bfloat16 or wider, within the bound.
No kernel may reach another device: no remote copies, remote signals or barrier semaphores. Data moves between devices by JAX's collectives and lax.ppermute only.
A program may use at most 64 MiB of HBM per device.

v0:
```python
import jax
import jax.numpy as jnp
from jax import lax
from jax.sharding import PartitionSpec as P

H = 128
P_SIZE = 64
G = 4
BLOCK = 128
epsilon = 1e-05
highest = lax.Precision.HIGHEST


def group_owners(first_head, head_count):
    head_ids = first_head + jnp.arange(head_count, dtype=jnp.int32)
    return head_ids // (H // G)


def group_pick(owners):
    return (owners[:, None] == jnp.arange(G, dtype=jnp.int32)[None, :]).astype(jnp.float32)


def scan_prompt(inputs, b_rows, c_rows, step_delta, rates, skip_gain, start_state, owners):
    length = inputs.shape[0]
    head_count = step_delta.shape[1]
    head_width = inputs.shape[1] // head_count
    states = b_rows.shape[1] // G
    blocks = length // BLOCK
    b_groups = b_rows.reshape(blocks, BLOCK, G, states)
    c_groups = c_rows.reshape(blocks, BLOCK, G, states)
    group_scores = jnp.einsum(
        "cign,cjgn->cijg", c_groups, b_groups, preferred_element_type=jnp.float32
    )
    head_scores = jnp.take(group_scores, owners, axis=3)
    b_head = jnp.take(b_groups, owners, axis=2).astype(jnp.float32)
    c_head = jnp.take(c_groups, owners, axis=2).astype(jnp.float32)
    values = inputs.astype(jnp.float32).reshape(blocks, BLOCK, head_count, head_width)
    block_delta = step_delta.reshape(blocks, BLOCK, head_count)
    decays = jnp.cumsum(-block_delta * rates, axis=1)
    causal_mask = (jnp.arange(BLOCK)[:, None] >= jnp.arange(BLOCK)[None, :])[None, :, :, None]
    spread = decays[:, :, None, :] - decays[:, None, :, :]
    weights = jnp.where(causal_mask, jnp.exp(jnp.where(causal_mask, spread, 0.0)), 0.0)
    scores = head_scores * weights * block_delta[:, None, :, :]
    inner_part = jnp.einsum("cijh,cjhp->cihp", scores, values, precision=highest)
    tail_decay = jnp.exp(decays[:, -1:, :] - decays) * block_delta
    block_states = jnp.einsum(
        "cjhn,cjhp->cnhp", b_head * tail_decay[..., None], values, precision=highest
    )
    block_totals = jnp.exp(decays[:, -1, :])

    def carry_step(carried, pieces):
        factor, fresh_term = pieces
        return (factor[None, :, None] * carried + fresh_term, carried)

    final_carry, starts = lax.scan(
        carry_step,
        start_state.reshape(states, head_count, head_width),
        (block_totals, block_states),
    )
    outer_part = (
        jnp.einsum("cihn,cnhp->cihp", c_head, starts, precision=highest)
        * jnp.exp(decays)[..., None]
    )
    result = inner_part + outer_part + skip_gain[None, None, :, None] * values
    return (
        result.reshape(length, head_count * head_width),
        final_carry.reshape(states, head_count * head_width),
    )


def gate_values(result, gate_rows):
    gate_rows = gate_rows.astype(jnp.float32)
    return result * gate_rows * jax.nn.sigmoid(gate_rows)


def select_heads(c_rows, owners):
    shape_front = c_rows.shape[:2]
    states = c_rows.shape[2] // G
    grouped = c_rows.reshape(shape_front[0], shape_front[1], G, states)
    return jnp.take(grouped, owners, axis=2)


def body(
    x_pre,
    z_pre,
    b_pre,
    c_pre,
    dt_pre,
    lengths,
    init_state,
    a_rates,
    dt_bias,
    skip_scale,
    norm_gain,
    x_dec,
    z_dec,
    b_dec,
    c_dec,
    dt_dec,
):
    heads_here = a_rates.shape[0]
    head_width = x_pre.shape[2] // heads_here
    first_head = lax.axis_index("head") * heads_here
    owners = group_owners(first_head, heads_here)
    picker = group_pick(owners)
    length = x_pre.shape[1]
    positions = jnp.arange(length, dtype=jnp.int32)
    valid_mask = (positions[None, :] < lengths[:, None]).astype(jnp.float32)
    step_delta = jax.nn.softplus(dt_pre + dt_bias) * valid_mask[:, :, None]

    def one_prompt(pieces):
        inputs, b_rows, c_rows, prompt_delta, start_state = pieces
        return scan_prompt(
            inputs, b_rows, c_rows, prompt_delta, a_rates, skip_scale, start_state, owners
        )

    result, final_carry = lax.map(one_prompt, (x_pre, b_pre, c_pre, step_delta, init_state))
    final_state = final_carry.astype(jnp.bfloat16)
    gated_rows = gate_values(result, z_pre)
    pre_totals = lax.psum(jnp.sum(gated_rows * gated_rows, axis=-1), "head")
    norm_scale = lax.rsqrt(pre_totals[:, :, None] / (H * P_SIZE) + epsilon)
    out_pre = (gated_rows * norm_scale * norm_gain * valid_mask[:, :, None]).astype(jnp.bfloat16)
    slots_here = x_dec.shape[0]
    prompt_count = x_dec.shape[1]
    prompts_here = final_state.shape[0]
    states = final_state.shape[1]
    cached = final_state.reshape(prompts_here, states, heads_here, head_width)
    queries = lax.all_to_all(c_dec, "sample", split_axis=1, concat_axis=0, tiled=True)
    c_head = select_heads(queries, owners)
    answers = jnp.einsum("sphn,pnhq->sphq", c_head, cached, preferred_element_type=jnp.float32)
    answers = answers.reshape(answers.shape[0], prompts_here, heads_here * head_width)
    state_reads = lax.all_to_all(
        answers.astype(jnp.bfloat16), "sample", split_axis=0, concat_axis=1, tiled=True
    ).astype(answers.dtype)
    state_reads = state_reads.reshape(slots_here, prompt_count, heads_here, head_width)
    c_groups = c_dec.astype(jnp.float32).reshape(slots_here, prompt_count, G, states)
    b_groups = b_dec.astype(jnp.float32).reshape(slots_here, prompt_count, G, states)
    cb_dot = jnp.einsum("spgn,spgn->spg", c_groups, b_groups, precision=highest)
    cb_dot = jnp.einsum("spg,hg->sph", cb_dot, picker, precision=highest)
    step_sizes = jax.nn.softplus(dt_dec + dt_bias)
    decay_rate = jnp.exp(-step_sizes * a_rates)
    values = x_dec.astype(jnp.float32).reshape(slots_here, prompt_count, heads_here, head_width)
    fresh_term = (
        decay_rate[..., None] * state_reads + (step_sizes * cb_dot + skip_scale)[..., None] * values
    )
    gated_dec = gate_values(
        fresh_term.reshape(slots_here, prompt_count, heads_here * head_width), z_dec
    )
    dec_totals = lax.psum(jnp.sum(gated_dec * gated_dec, axis=-1), "head")
    dec_scale = lax.rsqrt(dec_totals[:, :, None] / (H * P_SIZE) + epsilon)
    out_dec = (gated_dec * dec_scale * norm_gain).astype(jnp.bfloat16)
    return (out_pre, final_state, out_dec)


def solution(mesh):
    in_specs = (
        P(("rep", "sample"), None, "head"),
        P(("rep", "sample"), None, "head"),
        P(("rep", "sample"), None, None),
        P(("rep", "sample"), None, None),
        P(("rep", "sample"), None, "head"),
        P(("rep", "sample")),
        P(("rep", "sample"), None, "head"),
        P("head"),
        P("head"),
        P("head"),
        P("head"),
        P(("rep", "sample"), None, "head"),
        P(("rep", "sample"), None, "head"),
        P(("rep", "sample"), None, None),
        P(("rep", "sample"), None, None),
        P(("rep", "sample"), None, "head"),
    )
    out_specs = (
        P(("rep", "sample"), None, "head"),
        P(("rep", "sample"), None, "head"),
        P(("rep", "sample"), None, "head"),
    )
    return jax.shard_map(body, mesh=mesh, in_specs=in_specs, out_specs=out_specs, check_vma=False)
```

profile of v0, /device:TPU:0, one launch (start us, length us, event | category | flops | bytes accessed | tf_op | source)
XLA Modules:
  0.0 61.4 jit_solution(16359119723385610459)
XLA Ops:
  0.7 0.8 %copy.168 = bf16[1,4,512]{2,0,1:T(2,128)(2,1)S(1)} copy(bf16[1,4,512]{2,1,0:T(4,128)(2,1)} %param.32) | data formatting | bytes 8192 | tf_op args[14]
  1.9 0.7 %reduce.6 = bf16[4,512]{1,0:T(4,128)(2,1)S(1)} reduce(bf16[4,1,512]{2,1,0:T(2,128)(2,1)S(1)} %bitcast.142, bf16[]{:T(256)} %broadcast.360), dimensions={1}, to_apply=%bitcast.126.reduce_sub_computation | reduce | bytes 8194
  3.2 6.3 %all-to-all-start = ((bf16[4,2,256]{2,1,0:T(2,128)(2,1)}), bf16[4,2,256]{2,1,0:T(2,128)(2,1)}, u32[]{:S(2)}, u32[]{:S(2)}) async-start(bf16[4,2,256]{2,1,0:T(2,128)(2,1)} %reshape.510), calls=%async_computation | async-start | bytes 8192 | tf_op jit(solution)/shard_map/all_to_all | solution.py:128
  10.2 0.8 %negate_multiply_fusion = f32[1,128,32]{1,2,0:T(8,128)S(1)} fusion(f32[32]{0:T(128)} %param.25, f32[128]{0:T(128)S(1)} %compare_convert_fusion, f32[1,128,32]{1,2,0:T(8,128)} %param.22, f32[32]{0:T(128)} %param.26), kind=kLoop, calls=%fused_computation.73 | loop fusion | flops 40960 | bytes 33536 | tf_op jit(solution)/shard_map/while/body/eval_jaxpr/mul | solution.py:39
  11.9 0.6 iota_compare_fusion
  12.6 0.6 compare_select_fusion.3
  13.2 0.9 %reshape.439 = bf16[128,4,128]{2,1,0:T(4,128)(2,1)S(1)} reshape(bf16[1,128,512]{2,1,0:T(8,128)(2,1)} %param.21) | data formatting | bytes 262144 | tf_op jit(solution)/shard_map/reshape.21
  14.1 1.0 %copy.129 = bf16[1,128,512]{1,2,0:T(8,128)(2,1)S(1)} copy(bf16[1,128,512]{2,1,0:T(8,128)(2,1)} %param.21) | data formatting | bytes 262144 | tf_op args[3]
  15.2 2.0 %copy.127 = bf16[1,128,2048]{1,2,0:T(8,128)(2,1)} copy(bf16[1,128,2048]{2,1,0:T(8,128)(2,1)} %param.18) | data formatting | bytes 1048576 | tf_op args[0]
  17.2 1.2 %copy.133 = f32[1,128,2048]{1,2,0:T(8,128)} copy(bf16[1,128,2048]{2,1,0:T(8,128)(2,1)S(1)} %copy-done.2) | data formatting | bytes 1572864 | tf_op jit(solution)/shard_map/while/body/eval_jaxpr/convert_element_type | solution.py:37
  18.4 0.8 %copy.136 = bf16[1,128,512]{1,2,0:T(8,128)(2,1)} copy(bf16[1,128,512]{2,1,0:T(8,128)(2,1)S(1)} %copy-done.6) | data formatting | bytes 262144 | tf_op args[2]
  19.7 0.6 reshape.449
  20.3 0.7 %copy.125 = f32[128,32]{0,1:T(8,128)} copy(f32[128,32]{1,0:T(8,128)S(1)} %bitcast.135) | data formatting | bytes 32768 | tf_op jit(solution)/shard_map/while/body/eval_jaxpr/sub | solution.py:41
  21.0 0.6 pad_clamp_fusion.1
  21.7 0.6 pad_clamp_fusion
  22.8 0.7 %multiply_bitcast_fusion = (f32[128,32]{0,1:T(8,128)}, f32[128,32]{0,1:T(8,128)}) fusion(f32[1,128,32]{1,2,0:T(8,128)S(1)} %copy.138, f32[32]{0:T(128)S(1)} %slice_bitcast_fusion, f32[128]{0:T(128)S(1)} %compare_convert_fusion, f32[1,128,32]{1,2,0:T(8,128)S(1)} %copy-done.8, f32[32]{0:T(128)S(1)} %copy-done.18), kind=kLoop, calls=%fused_computation.72 | loop fusion | flops 40960 | bytes 66304 | tf_op jit(solution)/shard_map/while/body/eval_jaxpr/mul | solution.py:47
  23.7 0.8 %gather_fusion = f32[32,128,128]{1,2,0:T(8,128)S(1)} fusion(f32[128,128,4]{0,1,2:T(8,128)S(1)} %convolution_bitcast_fusion.1, s32[1024]{0:T(1024)} %pad_clamp_fusion.1), kind=kCustom, calls=%fused_computation.2 | custom fusion | bytes 4194432 | tf_op jit(solution)/shard_map/while/body/eval_jaxpr/jit(_take)/gather | solution.py:34
  24.5 1.9 %gather_fusion.2 = bf16[32,128,128]{2,1,0:T(8,128)(2,1)} fusion(bf16[128,4,128]{2,0,1:T(8,128)(2,1)S(1)} %bitcast.129, s32[1024]{0:T(1024)} %pad_clamp_fusion), kind=kCustom, calls=%fused_computation.clone | custom fusion | bytes 2097280 | tf_op jit(solution)/shard_map/while/body/eval_jaxpr/jit(_take)/gather | solution.py:36
  26.5 4.0 %fusion.12 = f32[1,128,32,64]{1,3,2,0:T(8,128)S(1)} fusion(bf16[128,32,64]{0,2,1:T(8,128)(2,1)} %bitcast.137, f32[32,128,128]{1,2,0:T(8,128)S(1)} %gather_fusion, f32[128,32]{0,1:T(8,128)S(1)} %copy-done.17, f32[128,32]{0,1:T(8,128)S(1)} %copy-done.12, pred[32]{0:T(512)(128)(4,1)S(1)} %copy-done.26, pred[128,128]{0,1:T(8,128)(4,1)S(1)} %copy-done.14), kind=kOutput, calls=%fused_computation.16 | convolution fusion | flops 405798912 | bytes 3719200 | tf_op jit(solution)/shard_map/while/body/eval_jaxpr/cijh,cjhp->cihp/dot_general | solution.py:44
  30.5 2.2 %fusion.17 = f32[1,128,32,64]{1,3,2,0:T(8,128)S(1)} fusion(f32[1,128,32,64]{1,3,2,0:T(8,128)S(1)} %fusion.12, f32[128,32,64]{0,2,1:T(8,128)S(1)} %bitcast.131, bf16[32,128,128]{2,1,0:T(8,128)(2,1)S(1)} %copy-done, f32[1,128,32,64]{1,3,2,0:T(8,128)S(1)} %bitcast.132, pred[32]{0:T(512)(128)(4,1)S(1)} %copy-done.26, f32[32]{0:T(128)S(1)} %copy-done.25, ...), kind=kOutput, calls=%fused_computation.20 | convolution fusion | flops 404226048 | bytes 5259424 | tf_op jit(solution)/shard_map/while/body/eval_jaxpr/cihn,cnhp->cihp/dot_general | solution.py:61
  33.8 1.8 %gather_fusion.3 = bf16[32,128,128]{2,1,0:T(8,128)(2,1)} fusion(bf16[128,4,128]{2,0,1:T(8,128)(2,1)S(1)} %bitcast.130, s32[1024]{0:T(1024)} %pad_clamp_fusion), kind=kCustom, calls=%fused_computation.1.clone | custom fusion | bytes 2097280 | tf_op jit(solution)/shard_map/while/body/eval_jaxpr/jit(_take)/gather | solution.py:35
  36.2 2.7 %fusion = f32[32,128,64]{1,2,0:T(8,128)S(1)} fusion(bf16[128,32,64]{0,2,1:T(8,128)(2,1)S(1)} %bitcast.138, bf16[32,128,128]{2,1,0:T(8,128)(2,1)} %gather_fusion.3, f32[128,32]{0,1:T(8,128)S(1)} %copy-done.16, pred[32]{0:T(512)(128)(4,1)S(1)} %copy-done.27), kind=kOutput, calls=%fused_computation.4 | convolution fusion | flops 404226048 | bytes 2637856 | tf_op jit(solution)/shard_map/while/body/eval_jaxpr/cjhn,cjhp->cnhp/dot_general | solution.py:46
  39.5 0.7 %reshape.511 = bf16[4,1,512]{2,1,0:T(2,128)(2,1)S(1)} reshape(bf16[4,2,256]{2,1,0:T(2,128)(2,1)} %all-to-all-done) | data formatting | bytes 8192
  40.2 0.7 %gather_fusion.1 = bf16[32,4,128]{2,1,0:T(4,128)(2,1)S(1)} fusion(bf16[4,4,128]{2,0,1:T(4,128)(2,1)S(1)} %bitcast.141, s32[1024]{0:T(1024)} %pad_clamp_fusion.1), kind=kCustom, calls=%fused_computation.3 | custom fusion | bytes 65664 | tf_op jit(solution)/shard_map/jit(_take)/gather | solution.py:80
  41.5 0.7 %reduce.7 = bf16[4,2048]{1,0:T(4,128)(2,1)S(1)} reduce(bf16[4,1,2048]{2,1,0:T(2,128)(2,1)S(1)} %convert_element_type.108, bf16[]{:T(256)} %broadcast.360), dimensions={1}, to_apply=%convert_element_type.108.reduce_sub_computation | reduce | bytes 32770 | tf_op jit(solution)/shard_map/convert_element_type | solution.py:133
  42.2 0.6 %reshape.512 = bf16[4,2,1024]{2,1,0:T(2,128)(2,1)} reshape(bf16[4,2048]{1,0:T(4,128)(2,1)S(1)} %reduce.7) | data formatting | bytes 32768
  42.8 5.1 %all-to-all-start.1 = ((bf16[4,2,1024]{2,1,0:T(2,128)(2,1)}), bf16[4,2,1024]{2,1,0:T(2,128)(2,1)S(1)}, u32[]{:S(2)}, u32[]{:S(2)}) async-start(bf16[4,2,1024]{2,1,0:T(2,128)(2,1)} %reshape.512), calls=%async_computation.1 | async-start | bytes 32768 | tf_op jit(solution)/shard_map/all_to_all | solution.py:132
  48.1 1.0 %copy.145 = bf16[1,128,2048]{2,1,0:T(8,128)(2,1)} copy(bf16[1,128,2048]{1,2,0:T(8,128)(2,1)S(1)} %fusion.26) | data formatting | bytes 1048576
  49.5 4.0 %all-to-all-done.1 = bf16[4,2,1024]{2,1,0:T(2,128)(2,1)S(1)} async-done(((bf16[4,2,1024]{2,1,0:T(2,128)(2,1)}), bf16[4,2,1024]{2,1,0:T(2,128)(2,1)S(1)}, u32[]{:S(2)}, u32[]{:S(2)}) %all-to-all-start.1) | async-done | bytes 16416 | tf_op jit(solution)/shard_map/all_to_all | solution.py:132
  53.8 5.6 %all-reduce = (f32[1,128]{1,0:T(1,128)S(1)}, f32[1,4]{1,0:T(1,128)S(1)}) all-reduce(f32[1,128]{1,0:T(1,128)S(1)} %bitcast.143, f32[1,4]{1,0:T(1,128)S(1)} %bitcast.144), channel_id=1, replica_groups=mesh['rep'=2,'sample'=4,'head'=4] {'head'}, use_global_device_ids=true, to_apply=%region_2.4 | all-reduce | flops 132 | bytes 1056 | tf_op jit(solution)/shard_map/psum | solution.py:120
  59.6 0.6 %copy.146 = bf16[1,4,2048]{2,1,0:T(4,128)(2,1)} copy(bf16[1,4,2048]{2,0,1:T(2,128)(2,1)S(1)} %multiply_convert_fusion.1) | data formatting | bytes 32768
  60.2 1.2 %multiply_convert_fusion = bf16[1,128,2048]{2,1,0:T(8,128)(2,1)} fusion(f32[128]{0:T(128)S(1)} %copy-done.21, f32[2048]{0:T(1024)S(1)} %copy-done.9, f32[128]{0:T(128)S(1)} %rsqrt_bitcast_fusion.1, f32[1,128,2048]{2,1,0:T(8,128)S(1)} %copy.134, bf16[1,128,2048]{2,1,0:T(8,128)(2,1)S(1)} %copy-done.3), kind=kLoop, calls=%fused_computation.41 | loop fusion | flops 2621440 | bytes 2106368 | tf_op jit(solution)/shard_map/convert_element_type | solution.py:122
  (100 shorter events, 6.9 us)
Async XLA Ops:
  0.6 16.6 %copy-start.2 = (bf16[1,128,2048]{2,1,0:T(8,128)(2,1)S(1)}, bf16[1,128,2048]{2,1,0:T(8,128)(2,1)}, u32[]{:S(2)}) copy-start(bf16[1,128,2048]{2,1,0:T(8,128)(2,1)} %param.18) | copy-start | bytes 1572868
  0.6 17.8 %copy-start.6 = (bf16[1,128,512]{2,1,0:T(8,128)(2,1)S(1)}, bf16[1,128,512]{2,1,0:T(8,128)(2,1)}, u32[]{:S(2)}) copy-start(bf16[1,128,512]{2,1,0:T(8,128)(2,1)} %param.20) | copy-start | bytes 393220
  1.9 17.8 %copy-start.13 = (bf16[1,4,512]{2,1,0:T(4,128)(2,1)S(1)}, bf16[1,4,512]{2,1,0:T(4,128)(2,1)}, u32[]{:S(2)}) copy-start(bf16[1,4,512]{2,1,0:T(4,128)(2,1)} %param.32) | copy-start | bytes 12292
  3.2 36.3 %all-to-all-start = ((bf16[4,2,256]{2,1,0:T(2,128)(2,1)}), bf16[4,2,256]{2,1,0:T(2,128)(2,1)}, u32[]{:S(2)}, u32[]{:S(2)}) async-start(bf16[4,2,256]{2,1,0:T(2,128)(2,1)} %reshape.510), calls=%async_computation | async-start | bytes 8192 | tf_op jit(solution)/shard_map/all_to_all | solution.py:128
  10.2 12.5 %copy-start.20 = (f32[128]{0:T(128)}, f32[128]{0:T(128)S(1)}, u32[]{:S(2)}) copy-start(f32[128]{0:T(128)S(1)} %compare_convert_fusion) | copy-start | bytes 1540
  12.6 9.8 %copy-start.4 = (f32[1,128,2048]{2,1,0:T(8,128)S(1)}, f32[1,128,2048]{2,1,0:T(8,128)}, u32[]{:S(2)}) copy-start(f32[1,128,2048]{2,1,0:T(8,128)} %param.24) | copy-start | bytes 3145732
  17.2 5.6 %copy-start.8 = (f32[1,128,32]{1,2,0:T(8,128)S(1)}, f32[1,128,32]{1,2,0:T(8,128)}, u32[]{:S(2)}) copy-start(f32[1,128,32]{1,2,0:T(8,128)} %param.22) | copy-start | bytes 49156
  17.2 5.6 %copy-start.18 = (f32[32]{0:T(128)S(1)}, f32[32]{0:T(128)}, u32[]{:S(2)}) copy-start(f32[32]{0:T(128)} %param.26) | copy-start | bytes 388
  24.5 2.0 %copy-start.12 = (f32[128,32]{0,1:T(8,128)S(1)}, f32[128,32]{0,1:T(8,128)}, u32[]{:S(2)}) copy-start(f32[128,32]{0,1:T(8,128)} %copy.125) | copy-start | bytes 49156
  24.5 2.0 %copy-start.14 = (pred[128,128]{0,1:T(8,128)(4,1)S(1)}, pred[128,128]{0,1:T(8,128)(4,1)}, u32[]{:S(2)}) copy-start(pred[128,128]{0,1:T(8,128)(4,1)} %iota_compare_fusion) | copy-start | bytes 49156
  24.5 2.0 %copy-start.17 = (f32[128,32]{0,1:T(8,128)S(1)}, f32[128,32]{0,1:T(8,128)}, u32[]{:S(2)}) copy-start(f32[128,32]{0,1:T(8,128)} %get-tuple-element.77) | copy-start | bytes 49156
  24.5 2.0 %copy-start.26 = (pred[32]{0:T(512)(128)(4,1)S(1)}, pred[32]{0:T(512)(128)(4,1)}, u32[]{:S(2)}) copy-start(pred[32]{0:T(512)(128)(4,1)} %compare_and_fusion) | copy-start | bytes 100
  26.5 4.0 %copy-start = (bf16[32,128,128]{2,1,0:T(8,128)(2,1)S(1)}, bf16[32,128,128]{2,1,0:T(8,128)(2,1)}, u32[]{:S(2)}) copy-start(bf16[32,128,128]{2,1,0:T(8,128)(2,1)} %gather_fusion.2) | copy-start | bytes 3145732
  26.5 4.0 %copy-start.1 = (f32[1,128,2048]{1,2,0:T(8,128)S(1)}, f32[1,128,2048]{1,2,0:T(8,128)}, u32[]{:S(2)}) copy-start(f32[1,128,2048]{1,2,0:T(8,128)} %copy.133) | copy-start | bytes 3145732
  26.5 4.0 %copy-start.25 = (f32[32]{0:T(128)S(1)}, f32[32]{0:T(128)}, u32[]{:S(2)}) copy-start(f32[32]{0:T(128)} %param.27) | copy-start | bytes 388
  32.7 0.9 %copy-start.7 = (bf16[1,128,512]{1,2,0:T(8,128)(2,1)S(1)}, bf16[1,128,512]{1,2,0:T(8,128)(2,1)}, u32[]{:S(2)}) copy-start(bf16[1,128,512]{1,2,0:T(8,128)(2,1)} %copy.136) | copy-start | bytes 393220
  32.7 2.8 %copy-start.28 = (f32[32]{0:T(128)S(1)}, f32[32]{0:T(128)}, u32[]{:S(2)}) copy-start(f32[32]{0:T(128)} %fusion.59) | copy-start | bytes 388
  32.8 3.0 %copy-start.22 = (bf16[1,4,512]{2,1,0:T(4,128)(2,1)S(1)}, bf16[1,4,512]{2,1,0:T(4,128)(2,1)}, u32[]{:S(2)}) copy-start(bf16[1,4,512]{2,1,0:T(4,128)(2,1)} %param.31) | copy-start | bytes 12292
  32.8 3.0 %copy-start.19 = (f32[32]{0:T(128)S(1)}, f32[32]{0:T(128)}, u32[]{:S(2)}) copy-start(f32[32]{0:T(128)} %param.26) | copy-start | bytes 388
  32.8 3.0 %copy-start.23 = (f32[32]{0:T(128)S(1)}, f32[32]{0:T(128)}, u32[]{:S(2)}) copy-start(f32[32]{0:T(128)} %param.25) | copy-start | bytes 388
  32.8 2.9 %copy-start.24 = (f32[1,4,32]{2,1,0:T(4,128)S(1)}, f32[1,4,32]{2,1,0:T(4,128)}, u32[]{:S(2)}) copy-start(f32[1,4,32]{2,1,0:T(4,128)} %param.33) | copy-start | bytes 1540
  33.1 2.6 %copy-start.3 = (bf16[1,128,2048]{2,1,0:T(8,128)(2,1)S(1)}, bf16[1,128,2048]{2,1,0:T(8,128)(2,1)}, u32[]{:S(2)}) copy-start(bf16[1,128,2048]{2,1,0:T(8,128)(2,1)} %param.19) | copy-start | bytes 1572868
  33.2 3.0 %copy-start.5 = (bf16[1,128,2048]{1,2,0:T(8,128)(2,1)S(1)}, bf16[1,128,2048]{1,2,0:T(8,128)(2,1)}, u32[]{:S(2)}) copy-start(bf16[1,128,2048]{1,2,0:T(8,128)(2,1)} %copy.127) | copy-start | bytes 1572868
  33.2 3.0 %copy-start.16 = (f32[128,32]{0,1:T(8,128)S(1)}, f32[128,32]{0,1:T(8,128)}, u32[]{:S(2)}) copy-start(f32[128,32]{0,1:T(8,128)} %get-tuple-element.76) | copy-start | bytes 49156
  33.2 3.0 %copy-start.27 = (pred[32]{0:T(512)(128)(4,1)S(1)}, pred[32]{0:T(512)(128)(4,1)}, u32[]{:S(2)}) copy-start(pred[32]{0:T(512)(128)(4,1)} %compare_and_fusion) | copy-start | bytes 100
  36.2 3.2 %copy-start.15 = (bf16[4,4,128]{2,1,0:T(4,128)(2,1)S(1)}, bf16[4,4,128]{2,1,0:T(4,128)(2,1)}, u32[]{:S(2)}) copy-start(bf16[4,4,128]{2,1,0:T(4,128)(2,1)} %reshape.449) | copy-start | bytes 12292
  39.0 9.0 %copy-start.29 = (s32[32]{0:T(128)S(1)}, s32[32]{0:T(128)}, u32[]{:S(2)}) copy-start(s32[32]{0:T(128)} %get-tuple-element.79) | copy-start | bytes 388
  39.0 14.6 %copy-start.10 = (bf16[1,4,2048]{2,1,0:T(4,128)(2,1)S(1)}, bf16[1,4,2048]{2,1,0:T(4,128)(2,1)}, u32[]{:S(2)}) copy-start(bf16[1,4,2048]{2,1,0:T(4,128)(2,1)} %param.30) | copy-start | bytes 49156
  39.0 14.6 %copy-start.11 = (bf16[1,4,2048]{2,1,0:T(4,128)(2,1)S(1)}, bf16[1,4,2048]{2,1,0:T(4,128)(2,1)}, u32[]{:S(2)}) copy-start(bf16[1,4,2048]{2,1,0:T(4,128)(2,1)} %param.29) | copy-start | bytes 49156
  39.0 20.5 %copy-start.9 = (f32[2048]{0:T(1024)S(1)}, f32[2048]{0:T(1024)}, u32[]{:S(2)}) copy-start(f32[2048]{0:T(1024)} %param.28) | copy-start | bytes 24580
  39.0 21.2 %copy-start.21 = (f32[128]{0:T(128)S(1)}, f32[128]{0:T(128)}, u32[]{:S(2)}) copy-start(f32[128]{0:T(128)} %copy-done.20) | copy-start | bytes 1540
  42.8 10.7 %all-to-all-start.1 = ((bf16[4,2,1024]{2,1,0:T(2,128)(2,1)}), bf16[4,2,1024]{2,1,0:T(2,128)(2,1)S(1)}, u32[]{:S(2)}, u32[]{:S(2)}) async-start(bf16[4,2,1024]{2,1,0:T(2,128)(2,1)} %reshape.512), calls=%async_computation.1 | async-start | bytes 32768 | tf_op jit(solution)/shard_map/all_to_all | solution.py:132
where the time goes:
time: 62.1 us; the launch traced here: 61.4 us
  local copies, waits for them, and re-layouts  20.3 us (33%)
  starting transfers between devices  11.4 us (18%)
  matrix products  9.71 us (16%)
  other arithmetic  8.5 us (14%)
  blocking collectives  5.63 us (9%)
  waiting for transfers between devices  4.02 us (6%)
  between operations  1.81 us (3%)
    unnamed x72, local copies, waits for them, and re-layouts  9.6 us
    all_to_all x1, starting transfers between devices, body(): lax.all_to_all(c_dec, 'sample', split_axis=1, concat_axis=0, tiled=True)  6.35 us
    psum x1, blocking collectives, body(): pre_totals = lax.psum(jnp.sum(gated_rows * gated_rows, axis=-1), 'head')  5.63 us
    all_to_all x1, starting transfers between devices, body(): lax.all_to_all(answers.astype(jnp.bfloat16), 'sample', split_axis=0, conc...  5.09 us
    all_to_all x1, waiting for transfers between devices, body(): lax.all_to_all(answers.astype(jnp.bfloat16), 'sample', split_axis=0, conc...  4.01 us
    dot_general x1, matrix products, scan_prompt(): jnp.einsum('cijh,cjhp->cihp', scores, values, precision=highest)  3.96 us
    dot_general x1, matrix products, scan_prompt(): jnp.einsum('cjhn,cjhp->cnhp', b_head * tail_decay[..., None], values, pre...  2.73 us
    dot_general x1, matrix products, scan_prompt(): jnp.einsum('cihn,cnhp->cihp', c_head, starts, precision=highest)  2.2 us
  transfers between devices with their start and end apart: 2, of which 1 were waited for; matrix products, arithmetic and copies ran while one was open for 49% of the time, Pallas kernels for 0%

commit v1 on v0

--- a/solution.py
+++ b/solution.py
@@ -125,7 +125,10 @@
     prompts_here = final_state.shape[0]
     states = final_state.shape[1]
     cached = final_state.reshape(prompts_here, states, heads_here, head_width)
-    queries = lax.all_to_all(c_dec, "sample", split_axis=1, concat_axis=0, tiled=True)
+    size = lax.axis_size("sample")
+    parts = jnp.stack(jnp.split(c_dec, size, axis=1), axis=0)
+    parts = lax.all_to_all(parts, "sample", split_axis=0, concat_axis=0)
+    queries = jnp.concatenate(parts, axis=0)
     c_head = select_heads(queries, owners)
     answers = jnp.einsum("sphn,pnhq->sphq", c_head, cached, preferred_element_type=jnp.float32)
     answers = answers.reshape(answers.shape[0], prompts_here, heads_here * head_width)

time: 62.1 us -> 64.5 us (1.039)
  local copies, waits for them, and re-layouts: 20.3 us -> 21.9 us
  other arithmetic: 8.5 us -> 9.29 us
    another operation x4 -> x6, local copies, waits for them, and re-layouts: 1.59 us -> 3.06 us
    unnamed x72 -> x64, local copies, waits for them, and re-layouts: 9.6 us -> 8.68 us
    mul x1, other arithmetic: 0.71 us -> 1.44 us  [scan_prompt(): b_head * tail_decay[..., None]]
    another operation x0 -> x2, other arithmetic: none -> 0.73 us  [body(): parts = jnp.stack(jnp.split(c_dec, size, axis=1), axis=0)]
    unnamed x1 -> x0, other arithmetic: 0.67 us -> none
  transfers between devices with their start and end apart: 2 -> 2, of which waited for: 1 -> 1; matrix products, arithmetic and copies ran while one was open for 49% -> 50% of each run, Pallas kernels for 0% -> 0%
where the time goes in v1:
time: 64.5 us; the launch traced here: 63.8 us
  local copies, waits for them, and re-layouts  21.9 us (34%)
  starting transfers between devices  11.4 us (18%)
  matrix products  9.73 us (15%)
  other arithmetic  9.29 us (14%)
  blocking collectives  5.63 us (9%)
  waiting for transfers between devices  4.02 us (6%)
  between operations  1.78 us (3%)
    unnamed x64, local copies, waits for them, and re-layouts  8.68 us
    all_to_all x1, starting transfers between devices, body(): parts = lax.all_to_all(parts, 'sample', split_axis=0, concat_axis=0)  6.35 us
    psum x1, blocking collectives, body(): pre_totals = lax.psum(jnp.sum(gated_rows * gated_rows, axis=-1), 'head')  5.63 us
    all_to_all x1, starting transfers between devices, body(): lax.all_to_all(answers.astype(jnp.bfloat16), 'sample', split_axis=0, conc...  5.09 us
    all_to_all x1, waiting for transfers between devices, body(): lax.all_to_all(answers.astype(jnp.bfloat16), 'sample', split_axis=0, conc...  4.01 us
    dot_general x1, matrix products, scan_prompt(): jnp.einsum('cijh,cjhp->cihp', scores, values, precision=highest)  3.96 us
    dot_general x1, matrix products, scan_prompt(): jnp.einsum('cjhn,cjhp->cnhp', b_head * tail_decay[..., None], values, pre...  2.73 us
    dot_general x1, matrix products, scan_prompt(): jnp.einsum('cihn,cnhp->cihp', c_head, starts, precision=highest)  2.2 us
  transfers between devices with their start and end apart: 2, of which 1 were waited for; matrix products, arithmetic and copies ran while one was open for 50% of the time, Pallas kernels for 0%

profile of v1, /device:TPU:0, one launch (start us, length us, event | category | flops | bytes accessed | tf_op | source)
XLA Modules:
  0.0 63.8 jit_solution(543395055968481401)
XLA Ops:
  0.7 0.9 %slice_bitcast_fusion.3 = (bf16[1,1,1,512]{3,2,1,0:T(2,128)(2,1)S(1)}, bf16[1,1,1,512]{3,2,1,0:T(2,128)(2,1)S(1)}, bf16[1,1,1,512]{3,2,1,0:T(2,128)(2,1)S(1)}, bf16[1,1,1,512]{3,2,1,0:T(2,128)(2,1)S(1)}) fusion(bf16[1,4,512]{2,1,0:T(4,128)(2,1)} %param.32), kind=kLoop, calls=%fused_computation.86 | loop fusion | bytes 8192 | tf_op jit(solution)/shard_map/stack | solution.py:129
  2.2 0.7 %reduce.5 = bf16[4,512]{1,0:T(4,128)(2,1)S(1)} reduce(bf16[4,1,1,512]{3,2,1,0:T(2,128)(2,1)S(1)} %pad_maximum_fusion, bf16[]{:T(256)} %broadcast.360), dimensions={1,2}, to_apply=%pad_maximum_fusion.reduce_sub_computation | reduce | bytes 8194 | tf_op jit(solution)/shard_map/stack | solution.py:129
  2.9 0.6 reshape.502
  3.5 6.3 %all-to-all-start = ((bf16[4,2,256]{2,1,0:T(2,128)(2,1)}), bf16[4,2,256]{2,1,0:T(2,128)(2,1)}, u32[]{:S(2)}, u32[]{:S(2)}) async-start(bf16[4,2,256]{2,1,0:T(2,128)(2,1)} %reshape.502), calls=%async_computation | async-start | bytes 8192 | tf_op jit(solution)/shard_map/all_to_all | solution.py:130
  11.0 0.8 %negate_multiply_fusion = f32[1,128,32]{1,2,0:T(8,128)S(1)} fusion(f32[32]{0:T(128)} %param.25, f32[128]{0:T(128)S(1)} %compare_convert_fusion, f32[1,128,32]{1,2,0:T(8,128)} %param.22, f32[32]{0:T(128)} %param.26), kind=kLoop, calls=%fused_computation.73 | loop fusion | flops 40960 | bytes 33536 | tf_op jit(solution)/shard_map/while/body/eval_jaxpr/mul | solution.py:39
  12.1 0.7 %copy.114 = f32[1,128,32]{1,2,0:T(8,128)} copy(f32[1,128,32]{2,1,0:T(8,128)S(1)} %reduce_window_sum.12) | data formatting | bytes 32768 | tf_op jit(solution)/shard_map/while/body/eval_jaxpr/jit(cumsum)/reduce_window_sum | solution.py:39
  13.9 0.6 iota_compare_fusion
  14.5 0.9 %reshape.432 = bf16[128,4,128]{2,1,0:T(4,128)(2,1)S(1)} reshape(bf16[1,128,512]{2,1,0:T(8,128)(2,1)} %param.21) | data formatting | bytes 262144 | tf_op jit(solution)/shard_map/reshape.21
  15.5 1.0 %copy.105 = bf16[1,128,512]{1,2,0:T(8,128)(2,1)S(1)} copy(bf16[1,128,512]{2,1,0:T(8,128)(2,1)} %param.21) | data formatting | bytes 262144 | tf_op args[3]
  17.1 2.0 %copy.103 = bf16[1,128,2048]{1,2,0:T(8,128)(2,1)} copy(bf16[1,128,2048]{2,1,0:T(8,128)(2,1)} %param.18) | data formatting | bytes 1048576 | tf_op args[0]
  19.1 1.2 %copy.109 = f32[1,128,2048]{1,2,0:T(8,128)} copy(bf16[1,128,2048]{2,1,0:T(8,128)(2,1)S(1)} %copy-done.2) | data formatting | bytes 1572864 | tf_op jit(solution)/shard_map/while/body/eval_jaxpr/convert_element_type | solution.py:37
  20.3 0.6 reshape.441
  21.5 0.8 %copy.112 = bf16[1,128,512]{1,2,0:T(8,128)(2,1)} copy(bf16[1,128,512]{2,1,0:T(8,128)(2,1)S(1)} %copy-done.6) | data formatting | bytes 262144 | tf_op args[2]
  22.3 0.6 pad_clamp_fusion.1
  22.9 0.7 %copy.101 = f32[128,32]{0,1:T(8,128)} copy(f32[128,32]{1,0:T(8,128)S(1)} %bitcast.138) | data formatting | bytes 32768 | tf_op jit(solution)/shard_map/while/body/eval_jaxpr/sub | solution.py:41
  24.9 0.8 %gather_fusion = f32[32,128,128]{1,2,0:T(8,128)S(1)} fusion(f32[128,128,4]{0,1,2:T(8,128)S(1)} %convolution_bitcast_fusion.1, s32[1024]{0:T(1024)} %pad_clamp_fusion.1), kind=kCustom, calls=%fused_computation.2 | custom fusion | bytes 4194432 | tf_op jit(solution)/shard_map/while/body/eval_jaxpr/jit(_take)/gather | solution.py:34
  25.8 1.4 %multiply_bitcast_fusion = (f32[128,32]{0,1:T(8,128)}, f32[128,32]{0,1:T(8,128)S(1)}) fusion(f32[1,128,32]{1,2,0:T(8,128)} %copy.114, f32[32]{0:T(128)} %slice_bitcast_fusion.4, f32[128]{0:T(128)} %copy-done.17, f32[1,128,32]{1,2,0:T(8,128)} %param.22, f32[32]{0:T(128)} %param.26), kind=kLoop, calls=%fused_computation.72 | loop fusion | flops 40960 | bytes 66304 | tf_op jit(solution)/shard_map/while/body/eval_jaxpr/mul | solution.py:47
  27.2 1.8 %gather_fusion.2 = bf16[32,128,128]{2,1,0:T(8,128)(2,1)} fusion(bf16[128,4,128]{2,0,1:T(8,128)(2,1)S(1)} %bitcast.132, s32[1024]{0:T(1024)} %pad_clamp_fusion), kind=kCustom, calls=%fused_computation.clone | custom fusion | bytes 2097280 | tf_op jit(solution)/shard_map/while/body/eval_jaxpr/jit(_take)/gather | solution.py:36
  29.0 4.0 %fusion.12 = f32[1,128,32,64]{1,3,2,0:T(8,128)S(1)} fusion(bf16[128,32,64]{0,2,1:T(8,128)(2,1)} %bitcast.140, f32[32,128,128]{1,2,0:T(8,128)S(1)} %gather_fusion, f32[128,32]{0,1:T(8,128)S(1)} %get-tuple-element.74, f32[128,32]{0,1:T(8,128)S(1)} %copy-done.12, pred[32]{0:T(512)(128)(4,1)S(1)} %copy-done.23, pred[128,128]{0,1:T(8,128)(4,1)S(1)} %copy-done.13), kind=kOutput, calls=%fused_computation.16 | convolution fusion | flops 405798912 | bytes 3719200 | tf_op jit(solution)/shard_map/while/body/eval_jaxpr/cijh,cjhp->cihp/dot_general | solution.py:44
  33.0 2.2 %fusion.17 = f32[1,128,32,64]{1,3,2,0:T(8,128)S(1)} fusion(f32[1,128,32,64]{1,3,2,0:T(8,128)S(1)} %fusion.12, f32[128,32,64]{0,2,1:T(8,128)S(1)} %bitcast.134, bf16[32,128,128]{2,1,0:T(8,128)(2,1)S(1)} %copy-done, f32[1,128,32,64]{1,3,2,0:T(8,128)S(1)} %bitcast.135, pred[32]{0:T(512)(128)(4,1)S(1)} %copy-done.23, f32[32]{0:T(128)S(1)} %copy-done.22, ...), kind=kOutput, calls=%fused_computation.20 | convolution fusion | flops 404226048 | bytes 5259424 | tf_op jit(solution)/shard_map/while/body/eval_jaxpr/cihn,cnhp->cihp/dot_general | solution.py:61
  36.4 1.8 %gather_fusion.3 = bf16[32,128,128]{2,1,0:T(8,128)(2,1)} fusion(bf16[128,4,128]{2,0,1:T(8,128)(2,1)S(1)} %bitcast.133, s32[1024]{0:T(1024)} %pad_clamp_fusion), kind=kCustom, calls=%fused_computation.1.clone | custom fusion | bytes 2097280 | tf_op jit(solution)/shard_map/while/body/eval_jaxpr/jit(_take)/gather | solution.py:35
  38.6 2.7 %fusion = f32[32,128,64]{1,2,0:T(8,128)S(1)} fusion(bf16[128,32,64]{0,2,1:T(8,128)(2,1)S(1)} %bitcast.141, bf16[32,128,128]{2,1,0:T(8,128)(2,1)} %gather_fusion.3, f32[128,32]{0,1:T(8,128)S(1)} %copy-done.15, pred[32]{0:T(512)(128)(4,1)S(1)} %copy-done.24), kind=kOutput, calls=%fused_computation.4 | convolution fusion | flops 404226048 | bytes 2637856 | tf_op jit(solution)/shard_map/while/body/eval_jaxpr/cjhn,cjhp->cnhp/dot_general | solution.py:46
  41.9 0.7 %reshape.503 = bf16[4,1,1,512]{3,2,1,0:T(2,128)(2,1)S(1)} reshape(bf16[4,2,256]{2,1,0:T(2,128)(2,1)} %all-to-all-done) | data formatting | bytes 8192
  42.6 0.7 %gather_fusion.1 = bf16[32,4,128]{2,1,0:T(4,128)(2,1)S(1)} fusion(bf16[4,4,128]{2,0,1:T(4,128)(2,1)S(1)} %bitcast.144, s32[1024]{0:T(1024)} %pad_clamp_fusion.1), kind=kCustom, calls=%fused_computation.3 | custom fusion | bytes 65664 | tf_op jit(solution)/shard_map/jit(_take)/gather | solution.py:80
  43.9 0.8 %reduce.6 = bf16[4,2048]{1,0:T(4,128)(2,1)S(1)} reduce(bf16[4,1,2048]{2,1,0:T(2,128)(2,1)S(1)} %convert_element_type.108, bf16[]{:T(256)} %broadcast.360), dimensions={1}, to_apply=%convert_element_type.108.reduce_sub_computation | reduce | bytes 32770 | tf_op jit(solution)/shard_map/convert_element_type | solution.py:136
  44.6 0.6 reshape.504
  45.3 5.1 %all-to-all-start.1 = ((bf16[4,2,1024]{2,1,0:T(2,128)(2,1)}), bf16[4,2,1024]{2,1,0:T(2,128)(2,1)S(1)}, u32[]{:S(2)}, u32[]{:S(2)}) async-start(bf16[4,2,1024]{2,1,0:T(2,128)(2,1)} %reshape.504), calls=%async_computation.1 | async-start | bytes 32768 | tf_op jit(solution)/shard_map/all_to_all | solution.py:135
  50.5 1.0 %copy.120 = bf16[1,128,2048]{2,1,0:T(8,128)(2,1)} copy(bf16[1,128,2048]{1,2,0:T(8,128)(2,1)S(1)} %fusion.26) | data formatting | bytes 1048576
  51.9 4.0 %all-to-all-done.1 = bf16[4,2,1024]{2,1,0:T(2,128)(2,1)S(1)} async-done(((bf16[4,2,1024]{2,1,0:T(2,128)(2,1)}), bf16[4,2,1024]{2,1,0:T(2,128)(2,1)S(1)}, u32[]{:S(2)}, u32[]{:S(2)}) %all-to-all-start.1) | async-done | bytes 16416 | tf_op jit(solution)/shard_map/all_to_all | solution.py:135
  56.2 5.6 %all-reduce = (f32[1,128]{1,0:T(1,128)S(1)}, f32[1,4]{1,0:T(1,128)S(1)}) all-reduce(f32[1,128]{1,0:T(1,128)S(1)} %bitcast.145, f32[1,4]{1,0:T(1,128)S(1)} %bitcast.146), channel_id=1, replica_groups=mesh['rep'=2,'sample'=4,'head'=4] {'head'}, use_global_device_ids=true, to_apply=%region_2.4 | all-reduce | flops 132 | bytes 1056 | tf_op jit(solution)/shard_map/psum | solution.py:120
  61.9 1.2 %multiply_convert_fusion = bf16[1,128,2048]{2,1,0:T(8,128)(2,1)} fusion(f32[128]{0:T(128)S(1)} %copy-done.18, f32[2048]{0:T(1024)S(1)} %copy-done.9, f32[128]{0:T(128)S(1)} %rsqrt_bitcast_fusion.1, f32[1,128,2048]{2,1,0:T(8,128)S(1)} %copy.110, bf16[1,128,2048]{2,1,0:T(8,128)(2,1)S(1)} %copy-done.3), kind=kLoop, calls=%fused_computation.41 | loop fusion | flops 2621440 | bytes 2106368 | tf_op jit(solution)/shard_map/convert_element_type | solution.py:122
  63.2 0.6 copy.121
  (95 shorter events, 8.5 us)
Async XLA Ops:
  0.6 19.7 %copy-start.8 = (bf16[1,4,512]{2,1,0:T(4,128)(2,1)S(1)}, bf16[1,4,512]{2,1,0:T(4,128)(2,1)}, u32[]{:S(2)}) copy-start(bf16[1,4,512]{2,1,0:T(4,128)(2,1)} %param.32) | copy-start | bytes 12292
  0.6 18.5 %copy-start.2 = (bf16[1,128,2048]{2,1,0:T(8,128)(2,1)S(1)}, bf16[1,128,2048]{2,1,0:T(8,128)(2,1)}, u32[]{:S(2)}) copy-start(bf16[1,128,2048]{2,1,0:T(8,128)(2,1)} %param.18) | copy-start | bytes 1572868
  0.7 20.8 %copy-start.6 = (bf16[1,128,512]{2,1,0:T(8,128)(2,1)S(1)}, bf16[1,128,512]{2,1,0:T(8,128)(2,1)}, u32[]{:S(2)}) copy-start(bf16[1,128,512]{2,1,0:T(8,128)(2,1)} %param.20) | copy-start | bytes 393220
  3.5 38.4 %all-to-all-start = ((bf16[4,2,256]{2,1,0:T(2,128)(2,1)}), bf16[4,2,256]{2,1,0:T(2,128)(2,1)}, u32[]{:S(2)}, u32[]{:S(2)}) async-start(bf16[4,2,256]{2,1,0:T(2,128)(2,1)} %reshape.502), calls=%async_computation | async-start | bytes 8192 | tf_op jit(solution)/shard_map/all_to_all | solution.py:130
  10.5 0.5 copy-start.17
  11.8 11.8 %copy-start.4 = (f32[1,128,2048]{2,1,0:T(8,128)S(1)}, f32[1,128,2048]{2,1,0:T(8,128)}, u32[]{:S(2)}) copy-start(f32[1,128,2048]{2,1,0:T(8,128)} %param.24) | copy-start | bytes 3145732
  25.7 3.3 %copy-start.12 = (f32[128,32]{0,1:T(8,128)S(1)}, f32[128,32]{0,1:T(8,128)}, u32[]{:S(2)}) copy-start(f32[128,32]{0,1:T(8,128)} %copy.101) | copy-start | bytes 49156
  25.7 3.3 %copy-start.13 = (pred[128,128]{0,1:T(8,128)(4,1)S(1)}, pred[128,128]{0,1:T(8,128)(4,1)}, u32[]{:S(2)}) copy-start(pred[128,128]{0,1:T(8,128)(4,1)} %iota_compare_fusion) | copy-start | bytes 49156
  25.7 3.3 %copy-start.23 = (pred[32]{0:T(512)(128)(4,1)S(1)}, pred[32]{0:T(512)(128)(4,1)}, u32[]{:S(2)}) copy-start(pred[32]{0:T(512)(128)(4,1)} %compare_and_fusion) | copy-start | bytes 100
  29.0 4.0 %copy-start = (bf16[32,128,128]{2,1,0:T(8,128)(2,1)S(1)}, bf16[32,128,128]{2,1,0:T(8,128)(2,1)}, u32[]{:S(2)}) copy-start(bf16[32,128,128]{2,1,0:T(8,128)(2,1)} %gather_fusion.2) | copy-start | bytes 3145732
  29.0 4.0 %copy-start.1 = (f32[1,128,2048]{1,2,0:T(8,128)S(1)}, f32[1,128,2048]{1,2,0:T(8,128)}, u32[]{:S(2)}) copy-start(f32[1,128,2048]{1,2,0:T(8,128)} %copy.109) | copy-start | bytes 3145732
  29.0 4.0 %copy-start.22 = (f32[32]{0:T(128)S(1)}, f32[32]{0:T(128)}, u32[]{:S(2)}) copy-start(f32[32]{0:T(128)} %param.27) | copy-start | bytes 388
  35.3 0.7 %copy-start.19 = (bf16[1,4,512]{2,1,0:T(4,128)(2,1)S(1)}, bf16[1,4,512]{2,1,0:T(4,128)(2,1)}, u32[]{:S(2)}) copy-start(bf16[1,4,512]{2,1,0:T(4,128)(2,1)} %param.31) | copy-start | bytes 12292
  35.3 0.7 %copy-start.16 = (f32[32]{0:T(128)S(1)}, f32[32]{0:T(128)}, u32[]{:S(2)}) copy-start(f32[32]{0:T(128)} %param.26) | copy-start | bytes 388
  35.3 0.7 %copy-start.20 = (f32[32]{0:T(128)S(1)}, f32[32]{0:T(128)}, u32[]{:S(2)}) copy-start(f32[32]{0:T(128)} %param.25) | copy-start | bytes 388
  35.3 0.7 %copy-start.21 = (f32[1,4,32]{2,1,0:T(4,128)S(1)}, f32[1,4,32]{2,1,0:T(4,128)}, u32[]{:S(2)}) copy-start(f32[1,4,32]{2,1,0:T(4,128)} %param.33) | copy-start | bytes 1540
  35.3 0.7 %copy-start.25 = (f32[32]{0:T(128)S(1)}, f32[32]{0:T(128)}, u32[]{:S(2)}) copy-start(f32[32]{0:T(128)} %fusion.59) | copy-start | bytes 388
  35.3 0.9 %copy-start.7 = (bf16[1,128,512]{1,2,0:T(8,128)(2,1)S(1)}, bf16[1,128,512]{1,2,0:T(8,128)(2,1)}, u32[]{:S(2)}) copy-start(bf16[1,128,512]{1,2,0:T(8,128)(2,1)} %copy.112) | copy-start | bytes 393220
  35.9 2.2 %copy-start.3 = (bf16[1,128,2048]{2,1,0:T(8,128)(2,1)S(1)}, bf16[1,128,2048]{2,1,0:T(8,128)(2,1)}, u32[]{:S(2)}) copy-start(bf16[1,128,2048]{2,1,0:T(8,128)(2,1)} %param.19) | copy-start | bytes 1572868
  35.9 2.6 %copy-start.5 = (bf16[1,128,2048]{1,2,0:T(8,128)(2,1)S(1)}, bf16[1,128,2048]{1,2,0:T(8,128)(2,1)}, u32[]{:S(2)}) copy-start(bf16[1,128,2048]{1,2,0:T(8,128)(2,1)} %copy.103) | copy-start | bytes 1572868
  36.0 2.6 %copy-start.15 = (f32[128,32]{0,1:T(8,128)S(1)}, f32[128,32]{0,1:T(8,128)}, u32[]{:S(2)}) copy-start(f32[128,32]{0,1:T(8,128)} %get-tuple-element.73) | copy-start | bytes 49156
  36.0 2.6 %copy-start.24 = (pred[32]{0:T(512)(128)(4,1)S(1)}, pred[32]{0:T(512)(128)(4,1)}, u32[]{:S(2)}) copy-start(pred[32]{0:T(512)(128)(4,1)} %compare_and_fusion) | copy-start | bytes 100
  38.6 3.2 %copy-start.14 = (bf16[4,4,128]{2,1,0:T(4,128)(2,1)S(1)}, bf16[4,4,128]{2,1,0:T(4,128)(2,1)}, u32[]{:S(2)}) copy-start(bf16[4,4,128]{2,1,0:T(4,128)(2,1)} %reshape.441) | copy-start | bytes 12292
  41.3 9.0 %copy-start.26 = (s32[32]{0:T(128)S(1)}, s32[32]{0:T(128)}, u32[]{:S(2)}) copy-start(s32[32]{0:T(128)} %get-tuple-element.80) | copy-start | bytes 388
  41.3 14.6 %copy-start.10 = (bf16[1,4,2048]{2,1,0:T(4,128)(2,1)S(1)}, bf16[1,4,2048]{2,1,0:T(4,128)(2,1)}, u32[]{:S(2)}) copy-start(bf16[1,4,2048]{2,1,0:T(4,128)(2,1)} %param.30) | copy-start | bytes 49156
  41.4 14.6 %copy-start.11 = (bf16[1,4,2048]{2,1,0:T(4,128)(2,1)S(1)}, bf16[1,4,2048]{2,1,0:T(4,128)(2,1)}, u32[]{:S(2)}) copy-start(bf16[1,4,2048]{2,1,0:T(4,128)(2,1)} %param.29) | copy-start | bytes 49156
  41.4 20.5 %copy-start.9 = (f32[2048]{0:T(1024)S(1)}, f32[2048]{0:T(1024)}, u32[]{:S(2)}) copy-start(f32[2048]{0:T(1024)} %param.28) | copy-start | bytes 24580
  41.4 20.5 %copy-start.18 = (f32[128]{0:T(128)S(1)}, f32[128]{0:T(128)}, u32[]{:S(2)}) copy-start(f32[128]{0:T(128)} %copy-done.17) | copy-start | bytes 1540
  45.3 10.7 %all-to-all-start.1 = ((bf16[4,2,1024]{2,1,0:T(2,128)(2,1)}), bf16[4,2,1024]{2,1,0:T(2,128)(2,1)S(1)}, u32[]{:S(2)}, u32[]{:S(2)}) async-start(bf16[4,2,1024]{2,1,0:T(2,128)(2,1)} %reshape.504), calls=%async_computation.1 | async-start | bytes 32768 | tf_op jit(solution)/shard_map/all_to_all | solution.py:135
